TPU v7x, 32 devices: a whole 2x2x4 slice. The times are simulated.
32 devices in a mesh: sub: 4 (over y, x), clu: 8 (over z, core).
Axes of the slice: x: 2, y: 2, z: 4, core: 2. Of those that a mesh axis runs over, the one named last changes fastest.
Arguments:
- right_side: float32 [65536, 256], P(('sub', 'clu')), may hold values from -6 to 6
- near_blocks: float32 [128, 3, 512, 512], P(('sub', 'clu')), may hold values from -0.15625 to 0.15625
- near_index: int32 [128, 3], P(('sub', 'clu')), may hold values from 0 to 127, as said below
- bases: float32 [128, 512, 128], P(('sub', 'clu')), may hold values from -0.25 to 0.25
- leaf_transfer: float32 [128, 128, 128], P(('sub', 'clu')), may hold values from -0.25 to 0.25
- cluster_transfer: float32 [32, 128, 128], P(('sub', 'clu')), may hold values from -0.1875 to 0.1875
- cluster_coupling: float32 [32, 4, 128, 128], P(('sub', 'clu')), may hold values from -0.25 to 0.25
- cluster_list: int32 [32, 4], P(('sub', 'clu')), may hold values from 0 to 31, as said below
- subtree_coupling: float32 [4, 3, 128, 128], P('sub'), may hold values from -0.3125 to 0.3125
- subtree_list: int32 [4, 3], P('sub'), may hold values from 0 to 3, as said below
Outputs:
- solution: float32 [65536, 256], P(('sub', 'clu'))
- residual: float32 [65536, 256], P(('sub', 'clu'))
Inputs may be any that keep to these rules, and one draw needn't show every extreme that they name: `near_index`: row g begins with g itself; its other entries are two different leaves within 2 leaves of g held by the same subtree; the first leaf of a cluster names the leaf before it, and the last the leaf after it, where those lie in the same subtree. `cluster_list`: the entries of a row are different clusters of the same subtree as the row's cluster, never that cluster itself. `subtree_list`: the entries of a row are different subtrees, never the row's own.
All inputs are finite; a program needn't handle non-finite values.
Results may differ from a plain program's by a relative error of at most 0.0001.
Values sent between devices are 32-bit elements; how exact they have to be, the bound alone decides.
A program may use at most 128 MiB of HBM per device.

v0:
```python
import jax
import jax.numpy as jnp
from jax import lax
from jax.sharding import PartitionSpec as P

REACH = 2
ITERS = 3


highest = lax.Precision.HIGHEST
spectrum_center = 3.0
spectrum_radius = 2.0
ridge_shift = 3.0


def with_halo(block, sides, width):
    for axis, dim in sides:
        count = lax.axis_size(axis)
        forward = [(i, i + 1) for i in range(count - 1)]
        backward = [(target, source) for source, target in forward]
        low = lax.ppermute(
            lax.slice_in_dim(block, block.shape[dim] - width, None, axis=dim), axis, forward
        )
        high = lax.ppermute(lax.slice_in_dim(block, 0, width, axis=dim), axis, backward)
        block = jnp.concatenate([low, block, high], axis=dim)
    return block


def body(
    right_side,
    near_blocks,
    near_index,
    bases,
    leaf_transfer,
    cluster_transfer,
    cluster_coupling,
    cluster_list,
    subtree_coupling,
    subtree_list,
):
    leaf_count = bases.shape[0]
    leaf_rows = bases.shape[1]
    columns = right_side.shape[1]
    clu_count = lax.axis_size("clu")
    device_index = lax.axis_index("sub") * clu_count + lax.axis_index("clu")
    first_leaf = device_index * leaf_count
    window_index = near_index - first_leaf + REACH
    neighbor_local = cluster_list[0] - lax.axis_index("sub") * clu_count
    transfer_all = lax.all_gather(cluster_transfer, "clu", axis=0, tiled=True)
    solution = jnp.zeros_like(right_side)
    residual = right_side
    update = right_side / spectrum_center
    weight_old = spectrum_radius / spectrum_center
    for turn_index in range(ITERS):
        solution = solution + update
        window = with_halo(update, (("clu", 0),), REACH * leaf_rows)
        near_leaves = window.reshape(leaf_count + 2 * REACH, leaf_rows, columns)
        picked = near_leaves[window_index]
        near = jnp.einsum("ljab,ljbr->lar", near_blocks, picked, precision=highest).reshape(
            -1, columns
        )
        leaves = update.reshape(leaf_count, leaf_rows, columns)
        leaf_coeffs = jnp.einsum("lak,lar->lkr", bases, leaves, precision=highest)
        own_coeffs = jnp.einsum("lkm,lkr->mr", leaf_transfer, leaf_coeffs, precision=highest)
        gathered = lax.all_gather(own_coeffs[None], "clu", axis=0, tiled=True)
        cluster_far = jnp.einsum(
            "jab,jbr->ar", cluster_coupling[0], gathered[neighbor_local], precision=highest
        )
        subtree_own = jnp.einsum("cka,ckr->ar", transfer_all, gathered, precision=highest)
        subtrees = lax.all_gather(subtree_own[None], "sub", axis=0, tiled=True)
        subtree_far = jnp.einsum(
            "jab,jbr->ar", subtree_coupling[0], subtrees[subtree_list[0]], precision=highest
        )
        combined = cluster_far + jnp.dot(cluster_transfer[0], subtree_far, precision=highest)
        lowered = jnp.einsum("lkm,mr->lkr", leaf_transfer, combined, precision=highest)
        far = jnp.einsum("lak,lkr->lar", bases, lowered, precision=highest).reshape(-1, columns)
        residual = residual - (ridge_shift * update + near + far)
        if turn_index + 1 < ITERS:
            weight_new = 1.0 / (2.0 * spectrum_center / spectrum_radius - weight_old)
            update = (
                weight_new * weight_old * update + 2.0 * weight_new / spectrum_radius * residual
            )
            weight_old = weight_new
    return (solution, residual)


def solution(mesh):
    placed = (
        P(("sub", "clu"), None),
        P(("sub", "clu"), None, None, None),
        P(("sub", "clu"), None),
        P(("sub", "clu"), None, None),
        P(("sub", "clu"), None, None),
        P(("sub", "clu"), None, None),
        P(("sub", "clu"), None, None, None),
        P(("sub", "clu"), None),
        P("sub", None, None, None),
        P("sub", None),
    )
    return jax.shard_map(
        body,
        mesh=mesh,
        in_specs=placed,
        out_specs=(P(("sub", "clu"), None), P(("sub", "clu"), None)),
        check_vma=False,
    )
```

profile of v0, /device:TPU:9, one launch (start us, length us, event | category | flops | bytes accessed | tf_op | source)
XLA Modules:
  0.0 335.5 jit_solution(6520470667724842446)
XLA Ops:
  7.2 1.9 broadcast_multiply_fusion
  9.1 3.5 %convolution_bitcast_fusion.11 = f32[4,128,256]{1,2,0:T(8,128)S(1)} fusion(f32[4,512,256]{2,1,0:T(8,128)S(1)} %bitcast.204, f32[4,512,128]{2,1,0:T(8,128)S(1)} %copy-done), kind=kOutput, calls=%fused_computation.35 | convolution fusion | flops 805306368 | bytes 3670016 | tf_op jit(solution)/shard_map/lak,lar->lkr/dot_general | solution.py:63
  12.6 1.2 convolution_bitcast_fusion.20
  13.9 1.5 fusion.20
  15.4 3.8 %collective-permute-start = (f32[1024,256]{1,0:T(8,128)}, f32[1024,256]{1,0:T(8,128)}, u32[]{:S(2)}, u32[]{:S(2)}) collective-permute-start(f32[1024,256]{1,0:T(8,128)} %get-tuple-element.10), channel_id=1, source_target_pairs={{0,1},{1,2},{2,3},{3,4},{4,5},{5,6},{6,7},{8,9},{9,10},{10,11},{11... | collective-permute-start | bytes 3145736 | tf_op jit(solution)/shard_map/ppermute | solution.py:21
  19.2 1.9 collective-permute-start.1
  21.3 32.8 %all_gather.22 = f32[8,128,128]{2,1,0:T(8,128)} all-gather(f32[1,128,128]{2,1,0:T(8,128)S(1)} %copy-done.6), channel_id=1, replica_groups=mesh['sub'=4,'clu'=8] {'clu'}, dimensions={0}, use_global_device_ids=true | all-gather | bytes 589824 | tf_op jit(solution)/shard_map/all_gather | solution.py:49
  54.1 3.9 %pad_maximum_fusion = f32[4096,256]{1,0:T(8,128)} fusion(f32[1024,256]{1,0:T(8,128)} %collective-permute-done.1, f32[2048,256]{1,0:T(8,128)S(1)} %broadcast_multiply_fusion, f32[1024,256]{1,0:T(8,128)} %collective-permute-done), kind=kLoop, calls=%fused_computation.9 | loop fusion | flops 2097152 | bytes 8388608 | tf_op jit(solution)/shard_map/concatenate | solution.py:25
  57.9 5.8 %gather_fusion = f32[12,512,256]{2,1,0:T(8,128)} fusion(f32[8,512,256]{2,1,0:T(8,128)} %bitcast.207, s32[1024]{0:T(1024)S(1)} %pad_clamp_fusion.2), kind=kCustom, calls=%fused_computation | custom fusion | bytes 12582960 | tf_op jit(solution)/shard_map/gather | solution.py:58
  63.7 24.0 %convolution_bitcast_fusion.5 = f32[4,512,256]{1,2,0:T(8,128)S(1)} fusion(f32[4,3,512,256]{3,2,1,0:T(8,128)} %bitcast.210, f32[4,3,512,512]{3,2,1,0:T(8,128)} %param.11), kind=kOutput, calls=%fused_computation.29 | convolution fusion | flops 9663676416 | bytes 20971520 | tf_op jit(solution)/shard_map/ljab,ljbr->lar/dot_general | solution.py:59
  87.7 2.2 copy.37
  89.9 1.6 copy.78
  91.5 1.8 convolution_bitcast_fusion.23
  93.4 13.0 %all-gather.1 = f32[512,256]{0,1:T(8,128)S(1)} all-gather(f32[128,256]{0,1:T(8,128)S(1)} %convolution_bitcast_fusion.23), channel_id=3, replica_groups=mesh['sub'=4,'clu'=8] {'sub'}, dimensions={0}, use_global_device_ids=true | all-gather | bytes 655360 | tf_op jit(solution)/shard_map/all_gather | solution.py:70
  106.3 1.0 copy.75
  107.9 1.6 gather_fusion.2
  110.4 1.0 convolution_bitcast_fusion.19
  112.3 1.8 convolution_bitcast_fusion.2
  114.1 1.8 copy.44
  115.9 3.3 multiply_add_fusion.1
  119.2 1.4 fusion.19
  120.6 7.2 %collective-permute-start.2 = (f32[1024,256]{1,0:T(8,128)}, f32[1024,256]{1,0:T(8,128)}, u32[]{:S(2)}, u32[]{:S(2)}) collective-permute-start(f32[1024,256]{1,0:T(8,128)} %get-tuple-element.8), channel_id=1, source_target_pairs={{0,1},{1,2},{2,3},{3,4},{4,5},{5,6},{6,7},{8,9},{9,10},{10,11},{11... | collective-permute-start | bytes 3145736 | tf_op jit(solution)/shard_map/ppermute | solution.py:21
  127.8 1.9 collective-permute-start.3
  129.8 3.5 %convolution_bitcast_fusion.9 = f32[4,128,256]{1,2,0:T(8,128)S(1)} fusion(f32[4,512,256]{2,1,0:T(8,128)S(1)} %bitcast.203, f32[4,512,128]{2,1,0:T(8,128)S(1)} %copy-done), kind=kOutput, calls=%fused_computation.33 | convolution fusion | flops 805306368 | bytes 3670016 | tf_op jit(solution)/shard_map/lak,lar->lkr/dot_general | solution.py:63
  133.2 1.2 convolution_bitcast_fusion.17
  134.7 5.2 %collective-permute-done.2 = f32[1024,256]{1,0:T(8,128)} collective-permute-done((f32[1024,256]{1,0:T(8,128)}, f32[1024,256]{1,0:T(8,128)}, u32[]{:S(2)}, u32[]{:S(2)}) %collective-permute-start.2) | collective-permute-done | bytes 1048608 | tf_op jit(solution)/shard_map/ppermute | solution.py:21
  139.9 5.2 %collective-permute-done.3 = f32[1024,256]{1,0:T(8,128)} collective-permute-done((f32[1024,256]{1,0:T(8,128)}, f32[1024,256]{1,0:T(8,128)}, u32[]{:S(2)}, u32[]{:S(2)}) %collective-permute-start.3) | collective-permute-done | bytes 1048608 | tf_op jit(solution)/shard_map/ppermute | solution.py:24
  145.1 3.9 %pad_maximum_fusion.1 = f32[4096,256]{1,0:T(8,128)} fusion(f32[1024,256]{1,0:T(8,128)} %collective-permute-done.3, f32[2048,256]{1,0:T(8,128)S(1)} %multiply_add_fusion.1, f32[1024,256]{1,0:T(8,128)} %collective-permute-done.2), kind=kLoop, calls=%fused_computation.10 | loop fusion | flops 2097152 | bytes 8388608 | tf_op jit(solution)/shard_map/concatenate | solution.py:25
  148.9 5.8 %gather_fusion.3 = f32[12,512,256]{2,1,0:T(8,128)} fusion(f32[8,512,256]{2,1,0:T(8,128)} %bitcast.208, s32[1024]{0:T(1024)S(1)} %pad_clamp_fusion.2), kind=kCustom, calls=%fused_computation.3 | custom fusion | bytes 12582960 | tf_op jit(solution)/shard_map/gather | solution.py:58
  154.7 25.3 %convolution_bitcast_fusion.4 = f32[4,512,256]{1,2,0:T(8,128)} fusion(f32[4,3,512,256]{3,2,1,0:T(8,128)} %bitcast.211, f32[4,3,512,512]{3,2,1,0:T(8,128)} %param.11), kind=kOutput, calls=%fused_computation.28 | convolution fusion | flops 9663676416 | bytes 20971520 | tf_op jit(solution)/shard_map/ljab,ljbr->lar/dot_general | solution.py:59
  180.0 3.1 copy.46
  183.2 2.5 copy.79
  185.7 3.8 %convolution_bitcast_fusion.22 = f32[128,256]{0,1:T(8,128)} fusion(f32[8,128,256]{2,1,0:T(8,128)} %bitcast.216, f32[8,128,128]{2,1,0:T(8,128)} %all_gather.22), kind=kOutput, calls=%fused_computation.52 | convolution fusion | flops 402653184 | bytes 1703936 | tf_op jit(solution)/shard_map/cka,ckr->ar/dot_general | solution.py:69
  189.5 2.6 gather_fusion.4
  192.1 12.1 %all-gather.3 = f32[512,256]{0,1:T(8,128)} all-gather(f32[128,256]{0,1:T(8,128)} %convolution_bitcast_fusion.22), channel_id=5, replica_groups=mesh['sub'=4,'clu'=8] {'sub'}, dimensions={0}, use_global_device_ids=true | all-gather | bytes 655360 | tf_op jit(solution)/shard_map/all_gather | solution.py:70
  204.2 2.0 copy.76
  206.2 2.4 gather_fusion.5
  208.6 1.9 convolution_bitcast_fusion.15
  210.4 2.1 convolution_bitcast_fusion.16
  213.4 3.2 convolution_bitcast_fusion.1
  216.6 2.9 copy.53
  219.5 6.2 %multiply_add_fusion = (f32[2048,256]{1,0:T(8,128)S(1)}, f32[2048,256]{1,0:T(8,128)}) fusion(f32[2048,256]{1,0:T(8,128)S(1)} %multiply_add_fusion.1, f32[4,512,256]{2,1,0:T(8,128)} %copy.53, f32[4,512,256]{2,1,0:T(8,128)} %copy.46, f32[2048,256]{1,0:T(8,128)} %param.10, f32[4,512,256]{2,1,0:T(8,128)} %copy.44, f32[4,512,256]{2,1,0:T(8,128)} %copy.37), kind=kLoop, calls=%fused_computation.21 | loop fusion | flops 5242880 | bytes 16777216 | tf_op jit(solution)/shard_map/add | solution.py:81
  225.7 1.6 fusion.18
  227.2 2.4 collective-permute-start.4
  229.7 1.9 collective-permute-start.5
  231.6 3.5 %convolution_bitcast_fusion.7 = f32[4,128,256]{1,2,0:T(8,128)S(1)} fusion(f32[4,512,256]{2,1,0:T(8,128)S(1)} %bitcast.205, f32[4,512,128]{2,1,0:T(8,128)S(1)} %copy-done), kind=kOutput, calls=%fused_computation.31 | convolution fusion | flops 805306368 | bytes 3670016 | tf_op jit(solution)/shard_map/lak,lar->lkr/dot_general | solution.py:63
  235.1 1.2 convolution_bitcast_fusion.14
  236.4 5.3 %collective-permute-done.4 = f32[1024,256]{1,0:T(8,128)} collective-permute-done((f32[1024,256]{1,0:T(8,128)}, f32[1024,256]{1,0:T(8,128)}, u32[]{:S(2)}, u32[]{:S(2)}) %collective-permute-start.4) | collective-permute-done | bytes 1048608 | tf_op jit(solution)/shard_map/ppermute | solution.py:21
  241.7 4.6 %collective-permute-done.5 = f32[1024,256]{1,0:T(8,128)} collective-permute-done((f32[1024,256]{1,0:T(8,128)}, f32[1024,256]{1,0:T(8,128)}, u32[]{:S(2)}, u32[]{:S(2)}) %collective-permute-start.5) | collective-permute-done | bytes 1048608 | tf_op jit(solution)/shard_map/ppermute | solution.py:24
  246.3 4.5 %pad_maximum_fusion.2 = f32[4096,256]{1,0:T(8,128)} fusion(f32[1024,256]{1,0:T(8,128)} %collective-permute-done.5, f32[2048,256]{1,0:T(8,128)} %copy-done.1, f32[1024,256]{1,0:T(8,128)} %collective-permute-done.4), kind=kLoop, calls=%fused_computation.11 | loop fusion | flops 2097152 | bytes 8388608 | tf_op jit(solution)/shard_map/concatenate | solution.py:25
  250.8 5.8 %gather_fusion.6 = f32[12,512,256]{2,1,0:T(8,128)} fusion(f32[8,512,256]{2,1,0:T(8,128)} %bitcast.206, s32[1024]{0:T(1024)S(1)} %pad_clamp_fusion.2), kind=kCustom, calls=%fused_computation.6 | custom fusion | bytes 12582960 | tf_op jit(solution)/shard_map/gather | solution.py:58
  256.6 25.6 %convolution_bitcast_fusion.3 = f32[4,512,256]{1,2,0:T(8,128)} fusion(f32[4,3,512,256]{3,2,1,0:T(8,128)} %bitcast.209, f32[4,3,512,512]{3,2,1,0:T(8,128)} %param.11), kind=kOutput, calls=%fused_computation.27 | convolution fusion | flops 9663676416 | bytes 20971520 | tf_op jit(solution)/shard_map/ljab,ljbr->lar/dot_general | solution.py:59
  282.2 3.0 copy.55
  285.3 2.5 copy.80
  287.8 3.8 %convolution_bitcast_fusion.21 = f32[128,256]{0,1:T(8,128)} fusion(f32[8,128,256]{2,1,0:T(8,128)} %bitcast.214, f32[8,128,128]{2,1,0:T(8,128)} %all_gather.22), kind=kOutput, calls=%fused_computation.51 | convolution fusion | flops 402653184 | bytes 1703936 | tf_op jit(solution)/shard_map/cka,ckr->ar/dot_general | solution.py:69
  291.6 2.6 gather_fusion.7
  294.2 13.1 %all-gather.5 = f32[512,256]{0,1:T(8,128)} all-gather(f32[128,256]{0,1:T(8,128)} %convolution_bitcast_fusion.21), channel_id=7, replica_groups=mesh['sub'=4,'clu'=8] {'sub'}, dimensions={0}, use_global_device_ids=true | all-gather | bytes 655360 | tf_op jit(solution)/shard_map/all_gather | solution.py:70
  307.4 2.0 copy.77
  309.4 2.4 gather_fusion.8
  311.8 1.9 convolution_bitcast_fusion.12
  313.6 2.1 convolution_bitcast_fusion.13
  316.6 3.1 convolution_bitcast_fusion
  319.7 2.9 copy.62
  322.6 6.2 %fusion = (f32[2048,256]{1,0:T(8,128)}, f32[2048,256]{1,0:T(8,128)}) fusion(f32[2048,256]{1,0:T(8,128)} %get-tuple-element.3, f32[4,512,256]{2,1,0:T(8,128)} %copy.62, f32[4,512,256]{2,1,0:T(8,128)} %copy.55, f32[2048,256]{1,0:T(8,128)S(1)} %multiply_add_fusion.1, f32[2048,256]{1,0:T(8,128)} %param.10), kind=kLoop, calls=%fused_computation.13 | loop fusion | flops 5242880 | bytes 14680064 | tf_op jit(solution)/shard_map/sub | solution.py:77
  (46 shorter events, 4.6 us)
Async XLA Ops:
  7.2 1.9 copy-start
  7.2 82.7 %all-gather.10.cloned.1.call-start = ((), (), s32[]{:S(2)}) async-start(), calls=%async_computation | async-start | bytes 1179648 | tf_op jit(solution)/shard_map/all_gather | solution.py:65
  9.1 3.5 %copy-start.2 = (f32[4,128,128]{2,1,0:T(8,128)S(1)}, f32[4,128,128]{2,1,0:T(8,128)}, u32[]{:S(2)}) copy-start(f32[4,128,128]{2,1,0:T(8,128)} %param.14) | copy-start | bytes 786436
  13.9 7.2 %copy-start.7 = (s32[4,3]{1,0:T(4,128)S(1)}, s32[4,3]{1,0:T(4,128)}, u32[]{:S(2)}) copy-start(s32[4,3]{1,0:T(4,128)} %param.12) | copy-start | bytes 148
  13.9 7.3 %copy-start.8 = (s32[1,3]{1,0:T(1,128)S(1)}, s32[1,3]{1,0:T(1,128)}, u32[]{:S(2)}) copy-start(s32[1,3]{1,0:T(1,128)} %param.19) | copy-start | bytes 40
  13.9 7.3 %copy-start.9 = (s32[1,4]{1,0:T(1,128)S(1)}, s32[1,4]{1,0:T(1,128)}, u32[]{:S(2)}) copy-start(s32[1,4]{1,0:T(1,128)} %param.17) | copy-start | bytes 52
  13.9 7.4 %copy-start.6 = (f32[1,128,128]{2,1,0:T(8,128)S(1)}, f32[1,128,128]{2,1,0:T(8,128)}, u32[]{:S(2)}) copy-start(f32[1,128,128]{2,1,0:T(8,128)} %param.15) | copy-start | bytes 196612
  13.9 169.2 %all-gather.12.cloned.1.call-start = ((), (), s32[]{:S(2)}) async-start(), calls=%async_computation.1 | async-start | bytes 1179648 | tf_op jit(solution)/shard_map/all_gather | solution.py:65
  15.4 38.7 %collective-permute-start = (f32[1024,256]{1,0:T(8,128)}, f32[1024,256]{1,0:T(8,128)}, u32[]{:S(2)}, u32[]{:S(2)}) collective-permute-start(f32[1024,256]{1,0:T(8,128)} %get-tuple-element.10), channel_id=1, source_target_pairs={{0,1},{1,2},{2,3},{3,4},{4,5},{5,6},{6,7},{8,9},{9,10},{10,11},{11... | collective-permute-start | bytes 3145736 | tf_op jit(solution)/shard_map/ppermute | solution.py:21
  19.2 34.9 %collective-permute-start.1 = (f32[1024,256]{1,0:T(8,128)}, f32[1024,256]{1,0:T(8,128)}, u32[]{:S(2)}, u32[]{:S(2)}) collective-permute-start(f32[1024,256]{1,0:T(8,128)} %get-tuple-element.11), channel_id=1, source_target_pairs={{1,0},{2,1},{3,2},{4,3},{5,4},{6,5},{7,6},{9,8},{10,9},{11,10},{12... | collective-permute-start | bytes 3145736 | tf_op jit(solution)/shard_map/ppermute | solution.py:24
  89.9 1.7 copy-start.3
  93.3 16.2 %copy-start.5 = (f32[1,3,128,128]{3,2,1,0:T(8,128)S(1)}, f32[1,3,128,128]{3,2,1,0:T(8,128)}, u32[]{:S(2)}) copy-start(f32[1,3,128,128]{3,2,1,0:T(8,128)} %param.18) | copy-start | bytes 589828
  93.3 17.0 %copy-start.4 = (f32[1,4,128,128]{3,2,1,0:T(8,128)S(1)}, f32[1,4,128,128]{3,2,1,0:T(8,128)}, u32[]{:S(2)}) copy-start(f32[1,4,128,128]{3,2,1,0:T(8,128)} %param.16) | copy-start | bytes 786436
  120.6 19.3 %collective-permute-start.2 = (f32[1024,256]{1,0:T(8,128)}, f32[1024,256]{1,0:T(8,128)}, u32[]{:S(2)}, u32[]{:S(2)}) collective-permute-start(f32[1024,256]{1,0:T(8,128)} %get-tuple-element.8), channel_id=1, source_target_pairs={{0,1},{1,2},{2,3},{3,4},{4,5},{5,6},{6,7},{8,9},{9,10},{10,11},{11... | collective-permute-start | bytes 3145736 | tf_op jit(solution)/shard_map/ppermute | solution.py:21
  127.8 17.2 %collective-permute-start.3 = (f32[1024,256]{1,0:T(8,128)}, f32[1024,256]{1,0:T(8,128)}, u32[]{:S(2)}, u32[]{:S(2)}) collective-permute-start(f32[1024,256]{1,0:T(8,128)} %get-tuple-element.9), channel_id=1, source_target_pairs={{1,0},{2,1},{3,2},{4,3},{5,4},{6,5},{7,6},{9,8},{10,9},{11,10},{12... | collective-permute-start | bytes 3145736 | tf_op jit(solution)/shard_map/ppermute | solution.py:24
  134.5 150.8 %all-gather.14.cloned.1.call-start = ((), (), s32[]{:S(2)}) async-start(), calls=%async_computation.2 | async-start | bytes 1179648 | tf_op jit(solution)/shard_map/all_gather | solution.py:65
  225.7 5.9 %copy-start.1 = (f32[2048,256]{1,0:T(8,128)}, f32[2048,256]{1,0:T(8,128)S(1)}, u32[]{:S(2)}) copy-start(f32[2048,256]{1,0:T(8,128)S(1)} %get-tuple-element.2) | copy-start | bytes 6291460
  227.2 14.5 %collective-permute-start.4 = (f32[1024,256]{1,0:T(8,128)}, f32[1024,256]{1,0:T(8,128)}, u32[]{:S(2)}, u32[]{:S(2)}) collective-permute-start(f32[1024,256]{1,0:T(8,128)} %get-tuple-element.6), channel_id=1, source_target_pairs={{0,1},{1,2},{2,3},{3,4},{4,5},{5,6},{6,7},{8,9},{9,10},{10,11},{11... | collective-permute-start | bytes 3145736 | tf_op jit(solution)/shard_map/ppermute | solution.py:21
  229.7 16.6 %collective-permute-start.5 = (f32[1024,256]{1,0:T(8,128)}, f32[1024,256]{1,0:T(8,128)}, u32[]{:S(2)}, u32[]{:S(2)}) collective-permute-start(f32[1024,256]{1,0:T(8,128)} %get-tuple-element.7), channel_id=1, source_target_pairs={{1,0},{2,1},{3,2},{4,3},{5,4},{6,5},{7,6},{9,8},{10,9},{11,10},{12... | collective-permute-start | bytes 3145736 | tf_op jit(solution)/shard_map/ppermute | solution.py:24
Sparse Core Ops, SparseCore 0:
  14.0 28.9 all-gather.9
  134.6 24.0 all-gather.11
  236.5 23.5 all-gather.13
where the time goes:
time: 341 us; the launch traced here: 336 us
  matrix products  119 us (35%)
  blocking collectives  70.9 us (21%)
  local copies, waits for them, and re-layouts  61.7 us (18%)
  other arithmetic  29.8 us (9%)
  waiting for transfers between devices  20.4 us (6%)
  starting transfers between devices  19.4 us (6%)
  between operations  14.4 us (4%)
    dot_general x3, matrix products, body(): jnp.einsum('ljab,ljbr->lar', near_blocks, picked, precision=highest)  74.9 us
    all_gather x3, blocking collectives, body(): subtrees = lax.all_gather(subtree_own[None], 'sub', axis=0, tiled=True)  38.2 us
    all_gather x1, blocking collectives, body(): transfer_all = lax.all_gather(cluster_transfer, 'clu', axis=0, tiled=True)  32.8 us
    gather x3, local copies, waits for them, and re-layouts, body(): picked = near_leaves[window_index]  17.4 us
    ppermute x3, starting transfers between devices, with_halo(): lax.ppermute(lax.slice_in_dim(block, block.shape[dim] - width, None, axis...  13.4 us
    concatenate x3, other arithmetic, with_halo(): block = jnp.concatenate([low, block, high], axis=dim)  12.2 us
    dot_general x3, matrix products, body(): leaf_coeffs = jnp.einsum('lak,lar->lkr', bases, leaves, precision=highest)  10.5 us
    ppermute x3, waiting for transfers between devices, with_halo(): lax.ppermute(lax.slice_in_dim(block, block.shape[dim] - width, None, axis...  10.5 us
  transfers between devices with their start and end apart: 9, of which 4 were waited for; matrix products, arithmetic and copies ran while one was open for 37% of the time, Pallas kernels for 0%

commit v1 on v0

v1 whole, which is shorter than its diff:
```python
import jax
import jax.numpy as jnp
from jax import lax
from jax.experimental import pallas as pl
from jax.experimental.pallas import tpu as pltpu
from jax.sharding import PartitionSpec as P

REACH = 2
ITERS = 3

spectrum_center = 3.0
spectrum_radius = 2.0
ridge_shift = 3.0

MESH = pl.DeviceIdType.MESH


def step_weights():
    weights = []
    old = spectrum_radius / spectrum_center
    for _ in range(ITERS - 1):
        new = 1.0 / (2.0 * spectrum_center / spectrum_radius - old)
        weights.append((new * old, 2.0 * new / spectrum_radius))
        old = new
    return weights


def split(x):
    high = x.astype(jnp.bfloat16)
    return high, (x - high.astype(jnp.float32)).astype(jnp.bfloat16)


def dot3(ah, al, bh, bl):
    def dot(a, b):
        return jnp.dot(a, b, preferred_element_type=jnp.float32)

    return dot(ah, bh) + (dot(ah, bl) + dot(al, bh))


def kernel(
    n_clu,
    n_sub,
    near_index,
    cluster_list,
    subtree_list,
    right_side,
    near_blocks,
    bases,
    leaf_transfer,
    cluster_transfer,
    cluster_coupling,
    subtree_coupling,
    solution,
    residual,
    update,
    halo,
    win_h,
    win_l,
    stage,
    near_h,
    near_l,
    w_h,
    w_l,
    wt_h,
    wt_l,
    t_all,
    tt_h,
    tt_l,
    coeffs,
    g_h,
    g_l,
    sub_all,
    s_h,
    s_l,
    c_far,
    stage_sem,
    halo_send,
    halo_recv,
    t_send,
    t_recv,
    c_send,
    c_recv,
    sub_send,
    sub_recv,
):
    leaf_count, leaf_rows, rank = bases.shape
    near_count = near_index.shape[1]
    ncc = cluster_list.shape[1]
    nsc = subtree_list.shape[1]
    sub = lax.axis_index("sub")
    clu = lax.axis_index("clu")
    lane = lax.rem(clu, 2)
    partner = clu + 1 - 2 * lane
    places = n_clu // 2
    has_low, has_high = clu >= 1, clu + 1 < n_clu
    has_down, has_up = clu >= 2, clu + 2 < n_clu
    first_leaf = (sub * n_clu + clu) * leaf_count

    barrier = pltpu.get_barrier_semaphore()

    def greet(device):
        pl.semaphore_signal(barrier, inc=1, device_id=device, device_id_type=MESH)

    for ok, where in ((has_low, clu - 1), (has_high, clu + 1), (has_down, clu - 2), (has_up, clu + 2)):

        @pl.when(ok)
        def _():
            greet({"clu": where})

    for k in range(1, n_sub):
        greet({"sub": lax.rem(sub + k, n_sub)})
    count = n_sub - 1
    for ok in (has_low, has_high, has_down, has_up):
        count = count + jnp.where(ok, 1, 0)
    pl.semaphore_wait(barrier, count)

    def stage_copy(i):
        slot = lax.rem(i, 2)
        return pltpu.make_async_copy(
            near_blocks.at[i // near_count, lax.rem(i, near_count)], stage.at[slot], stage_sem.at[slot]
        )

    stage_copy(0).start()
    stage_copy(1).start()

    class Chain:
        def __init__(self, view, send, recv):
            self.view, self.send, self.recv = view, send, recv

        def copy(self, block, way, target):
            return pltpu.make_async_remote_copy(
                src_ref=self.view(block),
                dst_ref=self.view(block),
                send_sem=self.send.at[way, block],
                recv_sem=self.recv(block),
                device_id={"clu": target},
                device_id_type=MESH,
            )

        def begin(self):
            @pl.when(has_up)
            def _():
                self.copy(clu, 0, clu + 2).start()

            @pl.when(has_down)
            def _():
                self.copy(clu, 1, clu - 2).start()

            self.copy(clu, 2, partner).start()

        def relay(self, t):
            @pl.when(clu - 2 * t >= 0)
            def _():
                block = clu - 2 * t
                self.copy(block, 2, partner).wait_recv()

                @pl.when(has_up)
                def _():
                    self.copy(block, 0, clu + 2).start()

                self.copy(block, 2, partner).start()

            @pl.when(clu + 2 * t < n_clu)
            def _():
                block = clu + 2 * t
                self.copy(block, 2, partner).wait_recv()

                @pl.when(has_down)
                def _():
                    self.copy(block, 1, clu - 2).start()

                self.copy(block, 2, partner).start()

        def finish(self):
            for q in range(places):
                self.copy(2 * q + 1 - lane, 2, partner).wait_recv()

        def drain(self):
            for q in range(places):
                block = 2 * q + lane

                @pl.when((block <= clu) & has_up)
                def _():
                    self.copy(block, 0, clu + 2).wait_send()

                @pl.when((block >= clu) & has_down)
                def _():
                    self.copy(block, 1, clu - 2).wait_send()

                self.copy(block, 2, partner).wait_send()

    t_chain = Chain(lambda b: t_all.at[b], t_send, lambda b: t_recv.at[b])

    def c_chain(it):
        return Chain(lambda b: coeffs.at[it, b], c_send, lambda b: c_recv.at[it, b])

    def halo_copy(it, side):
        return pltpu.make_async_remote_copy(
            src_ref=update.at[pl.ds(leaf_count - REACH if side == 0 else 0, REACH)],
            dst_ref=halo.at[it, side],
            send_sem=halo_send.at[side],
            recv_sem=halo_recv.at[it, side],
            device_id={"clu": clu + 1 if side == 0 else clu - 1},
            device_id_type=MESH,
        )

    def halo_start(it):
        @pl.when(has_high)
        def _():
            halo_copy(it, 0).start()

        @pl.when(has_low)
        def _():
            halo_copy(it, 1).start()

    def send_coeffs(it):
        total = None
        for leaf in range(leaf_count):
            term = dot3(wt_h[leaf], wt_l[leaf], win_h[REACH + leaf], win_l[REACH + leaf])
            total = term if total is None else total + term
        coeffs[it, clu] = total
        c_chain(it).begin()

    def first(leaf, carry):
        rows = pl.ds(leaf * leaf_rows, leaf_rows)
        r = right_side[rows, :]
        u = r / spectrum_center
        residual[rows, :] = r
        solution[rows, :] = u
        update[leaf] = u
        win_h[REACH + leaf], win_l[REACH + leaf] = split(u)
        return carry

    lax.fori_loop(0, leaf_count, first, 0)
    halo_start(0)
    t_all[clu] = cluster_transfer[0]
    t_chain.begin()

    def fold(leaf, carry):
        bh, bl = split(bases[leaf])
        lh, ll = split(leaf_transfer[leaf])
        w = dot3(bh, bl, lh, ll)
        w_h[leaf], w_l[leaf] = split(w)
        wt_h[leaf], wt_l[leaf] = split(w.T)
        return carry

    lax.fori_loop(0, leaf_count, fold, 0)
    send_coeffs(0)

    def unpack(i, carry):
        stage_copy(i).wait()
        near_h[i], near_l[i] = split(stage[lax.rem(i, 2)])

        @pl.when(i + 2 < leaf_count * near_count)
        def _():
            stage_copy(i + 2).start()

        return carry

    lax.fori_loop(0, leaf_count * near_count, unpack, 0)
    for t in range(1, places):
        t_chain.relay(t)
    t_chain.finish()
    for b in range(n_clu):
        tt_h[:, b * rank : (b + 1) * rank], tt_l[:, b * rank : (b + 1) * rank] = split(t_all[b].T)
    t_chain.drain()

    weights = step_weights()

    def near_product(leaf, j, where):
        i = leaf * near_count + j
        return dot3(near_h[i], near_l[i], win_h[where], win_l[where])

    def sub_copy(it, k, owner, target):
        return pltpu.make_async_remote_copy(
            src_ref=sub_all.at[it, owner],
            dst_ref=sub_all.at[it, owner],
            send_sem=sub_send.at[k],
            recv_sem=sub_recv.at[it, owner],
            device_id={"sub": target},
            device_id_type=MESH,
        )

    def iteration(it, carry):
        chain = c_chain(it)

        def own(leaf, carry):
            rows = pl.ds(leaf * leaf_rows, leaf_rows)
            residual[rows, :] = residual[rows, :] - (
                ridge_shift * update[leaf] + near_product(leaf, 0, REACH + leaf)
            )
            return carry

        chain.relay(1)
        lax.fori_loop(0, leaf_count, own, 0)
        for t in range(2, places):
            chain.relay(t)
        chain.finish()
        for b in range(n_clu):
            g_h[b], g_l[b] = split(coeffs[it, b])
        flat = (n_clu * rank, g_h.shape[2])
        sub_all[it, sub] = dot3(
            tt_h[...], tt_l[...], g_h[...].reshape(flat), g_l[...].reshape(flat)
        )
        for k in range(1, n_sub):
            sub_copy(it, k, sub, lax.rem(sub + k, n_sub)).start()
        far = None
        for j in range(ncc):
            at = jnp.clip(cluster_list[0, j] - sub * n_clu, 0, n_clu - 1)
            ah, al = split(cluster_coupling[0, j])
            term = dot3(ah, al, g_h[at], g_l[at])
            far = term if far is None else far + term
        c_far[...] = far

        @pl.when(has_low)
        def _():
            halo_copy(it, 0).wait_recv()
            for k in range(REACH):
                win_h[k], win_l[k] = split(halo[it, 0, k])

        @pl.when(has_high)
        def _():
            halo_copy(it, 1).wait_recv()
            for k in range(REACH):
                at = REACH + leaf_count + k
                win_h[at], win_l[at] = split(halo[it, 1, k])

        def others(leaf, carry):
            rows = pl.ds(leaf * leaf_rows, leaf_rows)
            total = None
            for j in range(1, near_count):
                where = jnp.clip(near_index[leaf, j] - first_leaf + REACH, 0, win_h.shape[0] - 1)
                term = near_product(leaf, j, where)
                total = term if total is None else total + term
            residual[rows, :] = residual[rows, :] - total
            return carry

        lax.fori_loop(0, leaf_count, others, 0)

        for k in range(1, n_sub):
            owner = lax.rem(sub + k, n_sub)
            sub_copy(it, k, owner, owner).wait_recv()
        for s in range(n_sub):
            s_h[s], s_l[s] = split(sub_all[it, s])
        top = None
        for j in range(nsc):
            at = subtree_list[0, j]
            ah, al = split(subtree_coupling[0, j])
            term = dot3(ah, al, s_h[at], s_l[at])
            top = term if top is None else top + term
        th, tl = split(top)
        ch, cl = split(cluster_transfer[0])
        down_h, down_l = split(c_far[...] + dot3(ch, cl, th, tl))
        for leaf in range(leaf_count):
            rows = pl.ds(leaf * leaf_rows, leaf_rows)
            residual[rows, :] = residual[rows, :] - dot3(w_h[leaf], w_l[leaf], down_h, down_l)

        chain.drain()
        for k in range(1, n_sub):
            sub_copy(it, k, sub, lax.rem(sub + k, n_sub)).wait_send()

        @pl.when(has_high)
        def _():
            halo_copy(it, 0).wait_send()

        @pl.when(has_low)
        def _():
            halo_copy(it, 1).wait_send()

        @pl.when(it + 1 < ITERS)
        def _():
            keep, gain = weights[-1]
            for k in range(len(weights) - 1):
                keep = jnp.where(it == k, weights[k][0], keep)
                gain = jnp.where(it == k, weights[k][1], gain)

            def advance(leaf, carry):
                rows = pl.ds(leaf * leaf_rows, leaf_rows)
                u = keep * update[leaf] + gain * residual[rows, :]
                update[leaf] = u
                solution[rows, :] = solution[rows, :] + u
                win_h[REACH + leaf], win_l[REACH + leaf] = split(u)
                return carry

            lax.fori_loop(0, leaf_count, advance, 0)
            send_coeffs(it + 1)
            halo_start(it + 1)

        return carry

    lax.fori_loop(0, ITERS, iteration, 0)


def body(
    right_side,
    near_blocks,
    near_index,
    bases,
    leaf_transfer,
    cluster_transfer,
    cluster_coupling,
    cluster_list,
    subtree_coupling,
    subtree_list,
):
    n_clu, n_sub = lax.axis_size("clu"), lax.axis_size("sub")
    leaf_count, leaf_rows, rank = bases.shape
    columns = right_side.shape[1]
    near_count = near_index.shape[1]
    blocks = leaf_count * near_count
    wide = leaf_count + 2 * REACH
    f32, bf16 = jnp.float32, jnp.bfloat16
    vmem = pl.BlockSpec(memory_space=pltpu.VMEM)
    smem = pl.BlockSpec(memory_space=pltpu.SMEM)
    hbm = pl.BlockSpec(memory_space=pl.ANY)
    dma = pltpu.SemaphoreType.DMA

    def run(*args):
        return kernel(n_clu, n_sub, *args)

    return pl.pallas_call(
        run,
        out_shape=(
            jax.ShapeDtypeStruct(right_side.shape, f32),
            jax.ShapeDtypeStruct(right_side.shape, f32),
        ),
        in_specs=[smem] * 3 + [vmem, hbm] + [vmem] * 5,
        out_specs=(vmem, vmem),
        scratch_shapes=[
            pltpu.VMEM((leaf_count, leaf_rows, columns), f32),
            pltpu.VMEM((ITERS, 2, REACH, leaf_rows, columns), f32),
            pltpu.VMEM((wide, leaf_rows, columns), bf16),
            pltpu.VMEM((wide, leaf_rows, columns), bf16),
            pltpu.VMEM((2, leaf_rows, leaf_rows), f32),
            pltpu.VMEM((blocks, leaf_rows, leaf_rows), bf16),
            pltpu.VMEM((blocks, leaf_rows, leaf_rows), bf16),
            pltpu.VMEM((leaf_count, leaf_rows, rank), bf16),
            pltpu.VMEM((leaf_count, leaf_rows, rank), bf16),
            pltpu.VMEM((leaf_count, rank, leaf_rows), bf16),
            pltpu.VMEM((leaf_count, rank, leaf_rows), bf16),
            pltpu.VMEM((n_clu, rank, rank), f32),
            pltpu.VMEM((rank, n_clu * rank), bf16),
            pltpu.VMEM((rank, n_clu * rank), bf16),
            pltpu.VMEM((ITERS, n_clu, rank, columns), f32),
            pltpu.VMEM((n_clu, rank, columns), bf16),
            pltpu.VMEM((n_clu, rank, columns), bf16),
            pltpu.VMEM((ITERS, n_sub, rank, columns), f32),
            pltpu.VMEM((n_sub, rank, columns), bf16),
            pltpu.VMEM((n_sub, rank, columns), bf16),
            pltpu.VMEM((rank, columns), f32),
            dma((2,)),
            dma((2,)),
            dma((ITERS, 2)),
            dma((3, n_clu)),
            dma((n_clu,)),
            dma((3, n_clu)),
            dma((ITERS, n_clu)),
            dma((n_sub,)),
            dma((ITERS, n_sub)),
        ],
        compiler_params=pltpu.CompilerParams(
            collective_id=0, has_side_effects=True, vmem_limit_bytes=63_000_000
        ),
    )(
        near_index,
        cluster_list,
        subtree_list,
        right_side,
        near_blocks,
        bases,
        leaf_transfer,
        cluster_transfer,
        cluster_coupling,
        subtree_coupling,
    )


def solution(mesh):
    placed = (
        P(("sub", "clu"), None),
        P(("sub", "clu"), None, None, None),
        P(("sub", "clu"), None),
        P(("sub", "clu"), None, None),
        P(("sub", "clu"), None, None),
        P(("sub", "clu"), None, None),
        P(("sub", "clu"), None, None, None),
        P(("sub", "clu"), None),
        P("sub", None, None, None),
        P("sub", None),
    )
    return jax.shard_map(
        body,
        mesh=mesh,
        in_specs=placed,
        out_specs=(P(("sub", "clu"), None), P(("sub", "clu"), None)),
        check_vma=False,
    )
```

time: 341 us -> 117 us (0.34)
  the two profiles are of different devices: /device:TPU:9 before, /device:TPU:0 now
where the time goes in v1:
time: 117 us
  Pallas kernels  111 us (95%)
  local copies, waits for them, and re-layouts  4.52 us (4%)
    pallas_call x1, Pallas kernels, body(): pl.pallas_call(run, out_shape=(jax.ShapeDtypeStruct(right_side.shape, f32...  111 us
    unnamed x4, local copies, waits for them, and re-layouts  4.52 us

profile of v1, /device:TPU:0, one launch (start us, length us, event | category | flops | bytes accessed | tf_op | source)
XLA Modules:
  0.0 116.5 jit_solution(13149660575386868976)
XLA Ops:
  0.6 111.4 %shard_map.113 = (f32[2048,256]{1,0:T(8,128)}, f32[2048,256]{1,0:T(8,128)}) custom-call(s32[4,3]{1,0:T(4,128)} %args_0_.4, s32[1,4]{1,0:T(1,128)} %args_1_.4, s32[1,3]{1,0:T(1,128)} %args_2_.4, f32[2048,256]{1,0:T(8,128)} %args_3_.4, f32[4,3,512,512]{3,2,1,0:T(8,128)} %args_4_.4, f32[4,512,128]{2,1,0:T(8,128)} %args_5_.4, f32[4,128,128]{2,1,0:T(8,128)} %args_6_.4, ...), custom_call_target="tpu_custom_call" | custom-call | tf_op jit(solution)/shard_map/pallas_call | solution.py:421
  112.0 0.0 copy-start
  112.0 3.2 %copy.14 = f32[2048,256]{1,0:T(8,128)} copy(f32[2048,256]{1,0:T(8,128)} %get-tuple-element.4) | data formatting | bytes 4194304
  115.2 0.0 copy-done
  115.2 1.3 %copy.15 = f32[2048,256]{1,0:T(8,128)} copy(f32[2048,256]{1,0:T(8,128)S(1)} %copy-done) | data formatting | bytes 4194304
Async XLA Ops:
  112.0 3.2 %copy-start = (f32[2048,256]{1,0:T(8,128)S(1)}, f32[2048,256]{1,0:T(8,128)}, u32[]{:S(2)}) copy-start(f32[2048,256]{1,0:T(8,128)} %get-tuple-element.5) | copy-start | bytes 6291460

commit v2 on v1

--- a/solution.py
+++ b/solution.py
@@ -7,6 +7,8 @@
 
 REACH = 2
 ITERS = 3
+PIECES = 1
+HALO_PIECES = 8
 
 spectrum_center = 3.0
 spectrum_radius = 2.0
@@ -73,6 +75,17 @@
     s_h,
     s_l,
     c_far,
+    c_near,
+    gram,
+    down_h,
+    down_l,
+    pending,
+    w_own,
+    w_beside,
+    wb_h,
+    wb_l,
+    down_own,
+    down_beside,
     stage_sem,
     halo_send,
     halo_recv,
@@ -82,6 +95,10 @@
     c_recv,
     sub_send,
     sub_recv,
+    w_send,
+    w_recv,
+    down_send,
+    down_recv,
 ):
     leaf_count, leaf_rows, rank = bases.shape
     near_count = near_index.shape[1]
@@ -127,99 +144,150 @@
         def __init__(self, view, send, recv):
             self.view, self.send, self.recv = view, send, recv
 
-        def copy(self, block, way, target):
+        def copy(self, block, piece, way, target):
             return pltpu.make_async_remote_copy(
-                src_ref=self.view(block),
-                dst_ref=self.view(block),
-                send_sem=self.send.at[way, block],
-                recv_sem=self.recv(block),
+                src_ref=self.view(block, piece),
+                dst_ref=self.view(block, piece),
+                send_sem=self.send.at[way, block, piece],
+                recv_sem=self.recv(block, piece),
                 device_id={"clu": target},
                 device_id_type=MESH,
             )
 
         def begin(self):
-            @pl.when(has_up)
-            def _():
-                self.copy(clu, 0, clu + 2).start()
-
-            @pl.when(has_down)
-            def _():
-                self.copy(clu, 1, clu - 2).start()
-
-            self.copy(clu, 2, partner).start()
-
-        def relay(self, t):
-            @pl.when(clu - 2 * t >= 0)
-            def _():
-                block = clu - 2 * t
-                self.copy(block, 2, partner).wait_recv()
+            for piece in range(PIECES):
 
                 @pl.when(has_up)
                 def _():
-                    self.copy(block, 0, clu + 2).start()
-
-                self.copy(block, 2, partner).start()
-
-            @pl.when(clu + 2 * t < n_clu)
-            def _():
-                block = clu + 2 * t
-                self.copy(block, 2, partner).wait_recv()
+                    self.copy(clu, piece, 0, clu + 2).start()
 
                 @pl.when(has_down)
                 def _():
-                    self.copy(block, 1, clu - 2).start()
-
-                self.copy(block, 2, partner).start()
+                    self.copy(clu, piece, 1, clu - 2).start()
+
+            for piece in range(PIECES):
+                self.copy(clu, piece, 2, partner).start()
+
+        def relay(self, t):
+            for piece in range(PIECES):
+
+                @pl.when(clu - 2 * t >= 0)
+                def _():
+                    block = clu - 2 * t
+                    self.copy(block, piece, 2, partner).wait_recv()
+
+                    @pl.when(has_up)
+                    def _():
+                        self.copy(block, piece, 0, clu + 2).start()
+
+                    self.copy(block, piece, 2, partner).start()
+
+                @pl.when(clu + 2 * t < n_clu)
+                def _():
+                    block = clu + 2 * t
+                    self.copy(block, piece, 2, partner).wait_recv()
+
+                    @pl.when(has_down)
+                    def _():
+                        self.copy(block, piece, 1, clu - 2).start()
+
+                    self.copy(block, piece, 2, partner).start()
 
         def finish(self):
             for q in range(places):
-                self.copy(2 * q + 1 - lane, 2, partner).wait_recv()
+                for piece in range(PIECES):
+                    self.copy(2 * q + 1 - lane, piece, 2, partner).wait_recv()
 
         def drain(self):
             for q in range(places):
                 block = 2 * q + lane
-
-                @pl.when((block <= clu) & has_up)
-                def _():
-                    self.copy(block, 0, clu + 2).wait_send()
-
-                @pl.when((block >= clu) & has_down)
-                def _():
-                    self.copy(block, 1, clu - 2).wait_send()
-
-                self.copy(block, 2, partner).wait_send()
-
-    t_chain = Chain(lambda b: t_all.at[b], t_send, lambda b: t_recv.at[b])
+                for piece in range(PIECES):
+
+                    @pl.when((block <= clu) & has_up)
+                    def _():
+                        self.copy(block, piece, 0, clu + 2).wait_send()
+
+                    @pl.when((block >= clu) & has_down)
+                    def _():
+                        self.copy(block, piece, 1, clu - 2).wait_send()
+
+                    self.copy(block, piece, 2, partner).wait_send()
+
+    part = rank // PIECES
+    t_chain = Chain(
+        lambda b, p: t_all.at[b, pl.ds(p * part, part)], t_send, lambda b, p: t_recv.at[b, p]
+    )
 
     def c_chain(it):
-        return Chain(lambda b: coeffs.at[it, b], c_send, lambda b: c_recv.at[it, b])
-
-    def halo_copy(it, side):
+        return Chain(
+            lambda b, p: coeffs.at[it, b, pl.ds(p * part, part)],
+            c_send,
+            lambda b, p: c_recv.at[it, b, p],
+        )
+
+    def edge(side):
+        return pl.ds(leaf_count - REACH if side == 0 else 0, REACH)
+
+    def beside(src, dst, send, recv, side):
         return pltpu.make_async_remote_copy(
-            src_ref=update.at[pl.ds(leaf_count - REACH if side == 0 else 0, REACH)],
-            dst_ref=halo.at[it, side],
-            send_sem=halo_send.at[side],
-            recv_sem=halo_recv.at[it, side],
+            src_ref=src,
+            dst_ref=dst,
+            send_sem=send,
+            recv_sem=recv,
             device_id={"clu": clu + 1 if side == 0 else clu - 1},
             device_id_type=MESH,
         )
 
-    def halo_start(it):
+    def w_copy(side):
+        return beside(w_own.at[edge(side)], w_beside.at[side], w_send.at[side], w_recv.at[side], side)
+
+    def down_copy(it, side):
+        return beside(
+            down_own.at[it],
+            down_beside.at[it, side],
+            down_send.at[side],
+            down_recv.at[it, side],
+            side,
+        )
+
+    def both_sides(act):
         @pl.when(has_high)
         def _():
-            halo_copy(it, 0).start()
+            act(0)
 
         @pl.when(has_low)
         def _():
-            halo_copy(it, 1).start()
-
-    def send_coeffs(it):
+            act(1)
+
+    per_leaf = HALO_PIECES // REACH
+    chunk = leaf_rows // per_leaf
+
+    def halo_copy(it, side, piece):
+        k, rows = piece // per_leaf, pl.ds(piece % per_leaf * chunk, chunk)
+        leaf = (leaf_count - REACH if side == 0 else 0) + k
+        return beside(
+            pending.at[leaf, rows],
+            halo.at[it, side, k, rows],
+            halo_send.at[side, piece],
+            halo_recv.at[it, side, piece],
+            side,
+        )
+
+    def halo_start(it, group):
+        begin, end = HALO_PIECES * group // places, HALO_PIECES * (group + 1) // places
+
+        def start(side):
+            for piece in range(begin, end):
+                halo_copy(it, side, piece).start()
+
+        both_sides(start)
+
+    def own_coeffs():
         total = None
         for leaf in range(leaf_count):
             term = dot3(wt_h[leaf], wt_l[leaf], win_h[REACH + leaf], win_l[REACH + leaf])
             total = term if total is None else total + term
-        coeffs[it, clu] = total
-        c_chain(it).begin()
+        return total
 
     def first(leaf, carry):
         rows = pl.ds(leaf * leaf_rows, leaf_rows)
@@ -228,24 +296,29 @@
         residual[rows, :] = r
         solution[rows, :] = u
         update[leaf] = u
+        pending[leaf] = u
         win_h[REACH + leaf], win_l[REACH + leaf] = split(u)
         return carry
 
     lax.fori_loop(0, leaf_count, first, 0)
-    halo_start(0)
     t_all[clu] = cluster_transfer[0]
     t_chain.begin()
+    halo_start(0, 0)
 
     def fold(leaf, carry):
         bh, bl = split(bases[leaf])
         lh, ll = split(leaf_transfer[leaf])
         w = dot3(bh, bl, lh, ll)
+        w_own[leaf] = w
         w_h[leaf], w_l[leaf] = split(w)
         wt_h[leaf], wt_l[leaf] = split(w.T)
+        gram[...] += dot3(wt_h[leaf], wt_l[leaf], w_h[leaf], w_l[leaf])
         return carry
 
+    gram[...] = jnp.zeros_like(gram)
     lax.fori_loop(0, leaf_count, fold, 0)
-    send_coeffs(0)
+    coeffs[0, clu] = own_coeffs()
+    c_chain(0).begin()
 
     def unpack(i, carry):
         stage_copy(i).wait()
@@ -257,15 +330,24 @@
 
         return carry
 
-    lax.fori_loop(0, leaf_count * near_count, unpack, 0)
+    blocks = leaf_count * near_count
     for t in range(1, places):
+        halo_start(0, t)
+        lax.fori_loop(blocks * (t - 1) // (places - 1), blocks * t // (places - 1), unpack, 0)
         t_chain.relay(t)
+        c_chain(0).relay(t)
     t_chain.finish()
     for b in range(n_clu):
         tt_h[:, b * rank : (b + 1) * rank], tt_l[:, b * rank : (b + 1) * rank] = split(t_all[b].T)
     t_chain.drain()
 
     weights = step_weights()
+
+    def pick_weight(it, which):
+        value = weights[-1][which]
+        for k in range(len(weights) - 1):
+            value = jnp.where(it == k, weights[k][which], value)
+        return value
 
     def near_product(leaf, j, where):
         i = leaf * near_count + j
@@ -291,10 +373,16 @@
             )
             return carry
 
-        chain.relay(1)
-        lax.fori_loop(0, leaf_count, own, 0)
-        for t in range(2, places):
-            chain.relay(t)
+        for t in range(1, places):
+
+            @pl.when(it > 0)
+            def _():
+                halo_start(it, t)
+                chain.relay(t)
+
+            begin, end = leaf_count * (t - 1) // (places - 1), leaf_count * t // (places - 1)
+            if begin < end:
+                lax.fori_loop(begin, end, own, 0)
         chain.finish()
         for b in range(n_clu):
             g_h[b], g_l[b] = split(coeffs[it, b])
@@ -312,18 +400,43 @@
             far = term if far is None else far + term
         c_far[...] = far
 
+        def arrive(side):
+            for piece in range(HALO_PIECES):
+                halo_copy(it, side, piece).wait_recv()
+            base = 0 if side == 0 else REACH + leaf_count
+
+            @pl.when(it == 0)
+            def _():
+                for k in range(REACH):
+                    win_h[base + k], win_l[base + k] = split(halo[it, side, k])
+
+            @pl.when(it == 1)
+            def _():
+                w_copy(side).wait_recv()
+                for k in range(REACH):
+                    wb_h[side, k], wb_l[side, k] = split(w_beside[side, k])
+
+            @pl.when(it >= 1)
+            def _():
+                past = it - 1
+                down_copy(past, side).wait_recv()
+                gain = pick_weight(past, 1)
+                dh, dl = split(down_beside[past, side])
+                for k in range(REACH):
+                    far = dot3(wb_h[side, k], wb_l[side, k], dh, dl)
+                    win_h[base + k], win_l[base + k] = split(halo[it, side, k] - gain * far)
+
         @pl.when(has_low)
         def _():
-            halo_copy(it, 0).wait_recv()
-            for k in range(REACH):
-                win_h[k], win_l[k] = split(halo[it, 0, k])
+            arrive(0)
 
         @pl.when(has_high)
         def _():
-            halo_copy(it, 1).wait_recv()
-            for k in range(REACH):
-                at = REACH + leaf_count + k
-                win_h[at], win_l[at] = split(halo[it, 1, k])
+            arrive(1)
+
+        @pl.when(it == 0)
+        def _():
+            both_sides(lambda side: w_copy(side).start())
 
         def others(leaf, carry):
             rows = pl.ds(leaf * leaf_rows, leaf_rows)
@@ -336,6 +449,35 @@
             return carry
 
         lax.fori_loop(0, leaf_count, others, 0)
+
+        keep, gain = pick_weight(it, 0), pick_weight(it, 1)
+
+        def sent(side):
+            for piece in range(HALO_PIECES):
+                halo_copy(it, side, piece).wait_send()
+
+        both_sides(sent)
+
+        @pl.when(it >= 1)
+        def _():
+            both_sides(lambda side: down_copy(it - 1, side).wait_send())
+
+        @pl.when(it == 1)
+        def _():
+            both_sides(lambda side: w_copy(side).wait_send())
+
+        @pl.when(it + 1 < ITERS)
+        def _():
+            def advance(leaf, carry):
+                rows = pl.ds(leaf * leaf_rows, leaf_rows)
+                u = keep * update[leaf] + gain * residual[rows, :]
+                pending[leaf] = u
+                win_h[REACH + leaf], win_l[REACH + leaf] = split(u)
+                return carry
+
+            lax.fori_loop(0, leaf_count, advance, 0)
+            halo_start(it + 1, 0)
+            c_near[...] = own_coeffs()
 
         for k in range(1, n_sub):
             owner = lax.rem(sub + k, n_sub)
@@ -350,41 +492,44 @@
             top = term if top is None else top + term
         th, tl = split(top)
         ch, cl = split(cluster_transfer[0])
-        down_h, down_l = split(c_far[...] + dot3(ch, cl, th, tl))
-        for leaf in range(leaf_count):
-            rows = pl.ds(leaf * leaf_rows, leaf_rows)
-            residual[rows, :] = residual[rows, :] - dot3(w_h[leaf], w_l[leaf], down_h, down_l)
+        down = c_far[...] + dot3(ch, cl, th, tl)
+        down_h[...], down_l[...] = split(down)
 
         chain.drain()
         for k in range(1, n_sub):
             sub_copy(it, k, sub, lax.rem(sub + k, n_sub)).wait_send()
 
-        @pl.when(has_high)
-        def _():
-            halo_copy(it, 0).wait_send()
-
-        @pl.when(has_low)
-        def _():
-            halo_copy(it, 1).wait_send()
+        def far_of(leaf):
+            return dot3(w_h[leaf], w_l[leaf], down_h[...], down_l[...])
 
         @pl.when(it + 1 < ITERS)
         def _():
-            keep, gain = weights[-1]
-            for k in range(len(weights) - 1):
-                keep = jnp.where(it == k, weights[k][0], keep)
-                gain = jnp.where(it == k, weights[k][1], gain)
-
-            def advance(leaf, carry):
+            gh, gl = split(gram[...])
+            coeffs[it + 1, clu] = c_near[...] - gain * dot3(gh, gl, down_h[...], down_l[...])
+            c_chain(it + 1).begin()
+            down_own[it] = down
+            both_sides(lambda side: down_copy(it, side).start())
+
+            def finish(leaf, carry):
                 rows = pl.ds(leaf * leaf_rows, leaf_rows)
-                u = keep * update[leaf] + gain * residual[rows, :]
+                far = far_of(leaf)
+                residual[rows, :] = residual[rows, :] - far
+                u = pending[leaf] - gain * far
                 update[leaf] = u
                 solution[rows, :] = solution[rows, :] + u
                 win_h[REACH + leaf], win_l[REACH + leaf] = split(u)
                 return carry
 
-            lax.fori_loop(0, leaf_count, advance, 0)
-            send_coeffs(it + 1)
-            halo_start(it + 1)
+            lax.fori_loop(0, leaf_count, finish, 0)
+
+        @pl.when(it + 1 == ITERS)
+        def _():
+            def finish(leaf, carry):
+                rows = pl.ds(leaf * leaf_rows, leaf_rows)
+                residual[rows, :] = residual[rows, :] - far_of(leaf)
+                return carry
+
+            lax.fori_loop(0, leaf_count, finish, 0)
 
         return carry
 
@@ -448,15 +593,30 @@
             pltpu.VMEM((n_sub, rank, columns), bf16),
             pltpu.VMEM((n_sub, rank, columns), bf16),
             pltpu.VMEM((rank, columns), f32),
+            pltpu.VMEM((rank, columns), f32),
+            pltpu.VMEM((rank, rank), f32),
+            pltpu.VMEM((rank, columns), bf16),
+            pltpu.VMEM((rank, columns), bf16),
+            pltpu.VMEM((leaf_count, leaf_rows, columns), f32),
+            pltpu.VMEM((leaf_count, leaf_rows, rank), f32),
+            pltpu.VMEM((2, REACH, leaf_rows, rank), f32),
+            pltpu.VMEM((2, REACH, leaf_rows, rank), bf16),
+            pltpu.VMEM((2, REACH, leaf_rows, rank), bf16),
+            pltpu.VMEM((ITERS - 1, rank, columns), f32),
+            pltpu.VMEM((ITERS - 1, 2, rank, columns), f32),
+            dma((2,)),
+            dma((2, HALO_PIECES)),
+            dma((ITERS, 2, HALO_PIECES)),
+            dma((3, n_clu, PIECES)),
+            dma((n_clu, PIECES)),
+            dma((3, n_clu, PIECES)),
+            dma((ITERS, n_clu, PIECES)),
+            dma((n_sub,)),
+            dma((ITERS, n_sub)),
             dma((2,)),
             dma((2,)),
-            dma((ITERS, 2)),
-            dma((3, n_clu)),
-            dma((n_clu,)),
-            dma((3, n_clu)),
-            dma((ITERS, n_clu)),
-            dma((n_sub,)),
-            dma((ITERS, n_sub)),
+            dma((2,)),
+            dma((ITERS - 1, 2)),
         ],
         compiler_params=pltpu.CompilerParams(
             collective_id=0, has_side_effects=True, vmem_limit_bytes=63_000_000

time: 117 us -> 105 us (0.90)
  Pallas kernels: 111 us -> 99.5 us
    pallas_call x1, Pallas kernels: 111 us -> 99.5 us  [body(): pl.pallas_call(run, out_shape=(jax.ShapeDtypeStruct(right_side.shape, f32...]
where the time goes in v2:
time: 105 us
  Pallas kernels  99.5 us (95%)
  local copies, waits for them, and re-layouts  4.52 us (4%)
    pallas_call x1, Pallas kernels, body(): pl.pallas_call(run, out_shape=(jax.ShapeDtypeStruct(right_side.shape, f32...  99.5 us
    unnamed x4, local copies, waits for them, and re-layouts  4.52 us

profile of v2, /device:TPU:0, one launch (start us, length us, event | category | flops | bytes accessed | tf_op | source)
XLA Modules:
  0.0 104.7 jit_solution(15037444009977129072)
XLA Ops:
  0.6 99.5 %shard_map.113 = (f32[2048,256]{1,0:T(8,128)}, f32[2048,256]{1,0:T(8,128)}) custom-call(s32[4,3]{1,0:T(4,128)} %args_0_.4, s32[1,4]{1,0:T(1,128)} %args_1_.4, s32[1,3]{1,0:T(1,128)} %args_2_.4, f32[2048,256]{1,0:T(8,128)} %args_3_.4, f32[4,3,512,512]{3,2,1,0:T(8,128)} %args_4_.4, f32[4,512,128]{2,1,0:T(8,128)} %args_5_.4, f32[4,128,128]{2,1,0:T(8,128)} %args_6_.4, ...), custom_call_target="tpu_custom_call" | custom-call | tf_op jit(solution)/shard_map/pallas_call | solution.py:566
  100.2 0.0 copy-start
  100.2 3.2 %copy.14 = f32[2048,256]{1,0:T(8,128)} copy(f32[2048,256]{1,0:T(8,128)} %get-tuple-element.4) | data formatting | bytes 4194304
  103.4 0.0 copy-done
  103.4 1.3 %copy.15 = f32[2048,256]{1,0:T(8,128)} copy(f32[2048,256]{1,0:T(8,128)S(1)} %copy-done) | data formatting | bytes 4194304
Async XLA Ops:
  100.2 3.2 %copy-start = (f32[2048,256]{1,0:T(8,128)S(1)}, f32[2048,256]{1,0:T(8,128)}, u32[]{:S(2)}) copy-start(f32[2048,256]{1,0:T(8,128)} %get-tuple-element.5) | copy-start | bytes 6291460
